TPU v7x, 128 devices: a whole 4x4x4 slice. The times are simulated.
128 devices in a mesh: atom: 16 (over y, x), mode: 8 (over z, core).
Axes of the slice: x: 4, y: 4, z: 4, core: 2. Of those that a mesh axis runs over, the one named last changes fastest.
Arguments:
- eigvec: bfloat16 [3, 4096, 2048], P(None, 'atom', 'mode'), may hold values from -0.0546875 to 0.0546875
- force: float32 [3, 3, 16, 4096], P(None, None, None, 'atom'), may hold values from -12 to 12
- bond: float32 [3, 16, 4096], P(None, None, 'atom'), may hold values from -6 to 6
- nbr: int32 [16, 4096], P(None, 'atom'), may hold values from 0 to 4095, as said below
- band: int32 [2, 2048], P(None, 'mode'), may hold values from 0 to 2048, as said below
- freq: float32 [2048], P('mode'), may hold values from 0.5 to 4, as said below
Outputs:
- diffusivity: float32 [2048], P('mode')
- conductivity: float32 [2048], P('mode')
Inputs may be any that keep to these rules, and one draw needn't show every extreme that they name: `nbr`: each entry is an atom whose position in atom order differs from that of its own atom by 1 to 128, counted cyclically over the 4096 atoms; the distance 128 occurs in every draw. For every mode i: max(0, i - 128) <= band[0, i] <= i < band[1, i] <= min(2048, i + 129); both outer limits are reached at some mode. `freq`: strictly increasing along the modes.
All inputs are finite; a program needn't handle non-finite values.
Results may differ from a plain program's by a relative error of at most 0.00057.
Values may be sent and summed in bfloat16 or wider, within the bound.
A program may use at most 64 MiB of HBM per device.

v0:
```python
import math
import jax
import jax.numpy as jnp
from jax import lax
from jax.sharding import PartitionSpec as P

ATOM_DEV = 256
MODE_DEV = 256
RIM = 128
HALF = 128
BROAD = 128


def extended(shard, sides, width, wrap):
    for axis, dim in sides:
        size, length = (lax.axis_size(axis), shard.shape[dim])
        up = [(i, (i + 1) % size) for i in range(size if wrap else size - 1)]
        down = [(j, i) for i, j in up]
        last = lax.slice_in_dim(shard, length - width, length, axis=dim)
        first = lax.slice_in_dim(shard, 0, width, axis=dim)
        before = lax.ppermute(last, axis, up)
        after = lax.ppermute(first, axis, down)
        shard = jnp.concatenate([before, shard, after], axis=dim)
    return shard


def prefix(part, axis, combine, identity):
    place = lax.axis_index(axis)
    gathered = lax.all_gather(part, axis)
    state = jnp.zeros_like(part) + jnp.asarray(identity, part.dtype)

    def one(lap, state):
        return combine(state, lax.dynamic_index_in_dim(gathered, lap, 0, False))

    return lax.fori_loop(0, place, one, state)


def capacity_of(spectral):
    return spectral * spectral * jnp.exp(spectral) / jnp.expm1(spectral) ** 2


def pair_weight(own_freq, partner_freq, own_ids, partner_ids, lower_end, upper_end, broaden):
    inside = (
        (partner_ids[:, None] >= lower_end[None, :])
        & (partner_ids[:, None] < upper_end[None, :])
        & (partner_ids[:, None] != own_ids[None, :])
    )
    detune = own_freq[None, :] - partner_freq[:, None]
    lorentz = broaden / math.pi / (detune * detune + broaden * broaden)
    factor = (own_freq[None, :] + partner_freq[:, None]) ** 2 / (
        4.0 * own_freq[None, :] * partner_freq[:, None]
    )
    return jnp.where(inside, lorentz * factor, 0.0)


def add_totals(earlier, later):
    return earlier + later


def body(eigvec, force, bond, nbr, band, freq):
    atom_count = ATOM_DEV * lax.axis_size("atom")
    mode_count = MODE_DEV * lax.axis_size("mode")
    partner_span = MODE_DEV + 2 * HALF
    spectrum = lax.all_gather(freq, "mode", axis=0, tiled=True)
    atom_rows = extended(eigvec, (("atom", 1),), RIM, True)
    band_rows = extended(eigvec, (("mode", 2),), HALF, False)
    row_major = jnp.transpose(atom_rows, (1, 0, 2))
    domain = lax.axis_index("atom")
    local_ids = (nbr - domain * ATOM_DEV + RIM + atom_count) % atom_count
    block_size = min(512, ATOM_DEV)
    gathered = jnp.take(row_major, local_ids, axis=0)
    coupling = (bond[:, None, None, :, 0:block_size] * force[None, :, :, :, 0:block_size]).astype(
        jnp.bfloat16
    )
    block_image = jnp.einsum(
        "kcdna,nadi->kcai", coupling, gathered, preferred_element_type=jnp.float32
    )
    pieces = block_image.astype(jnp.bfloat16)
    pair_terms = jnp.einsum("caj,kcai->kji", band_rows, pieces, preferred_element_type=jnp.float32)
    mode_block = lax.axis_index("mode")
    mode_start = mode_block * MODE_DEV
    broaden = BROAD * (jnp.max(spectrum) - jnp.min(spectrum)) / (mode_count - 1)
    padded_freq = jnp.pad(spectrum, (HALF, HALF), constant_values=1.0)
    partner_freq = lax.dynamic_slice_in_dim(padded_freq, mode_start, partner_span)
    partner_ids = mode_start - HALF + jnp.arange(partner_span, dtype=jnp.int32)
    own_ids = mode_start + jnp.arange(MODE_DEV, dtype=jnp.int32)
    weight = pair_weight(freq, partner_freq, own_ids, partner_ids, band[0], band[1], broaden)
    summed_pair = lax.psum(pair_terms, "atom")
    strength = jnp.sum(summed_pair * summed_pair, axis=0)
    row_sums = jnp.sum(weight * strength, axis=0)
    diffusivity = math.pi / (3.0 * freq * freq) * row_sums
    running = jnp.cumsum(capacity_of(freq) * diffusivity)
    device_total = running[-1]
    earlier_sum = prefix(device_total, "mode", add_totals, jnp.float32(0.0))
    conductivity = (earlier_sum + running) / MODE_DEV
    return (diffusivity, conductivity)


def solution(mesh):
    in_specs = (
        P(None, "atom", "mode"),
        P(None, None, None, "atom"),
        P(None, None, "atom"),
        P(None, "atom"),
        P(None, "mode"),
        P("mode"),
    )
    out_specs = (P("mode"), P("mode"))
    return jax.shard_map(body, mesh=mesh, in_specs=in_specs, out_specs=out_specs, check_vma=False)
```

profile of v0, /device:TPU:97, one launch (start us, length us, event | category | flops | bytes accessed | tf_op | source)
XLA Modules:
  0.0 190.9 jit_solution(17926169755393144528)
XLA Ops:
  7.2 0.0 copy-start
  7.2 0.0 copy-start.3
  7.2 0.0 copy-start.2
  7.2 0.0 all-reduce.4.cloned.1.call-start
  7.2 1.4 copy.12
  8.6 0.0 copy-start.4
  8.6 0.2 fusion.21
  8.8 5.0 %collective-permute-start.1 = (bf16[3,128,256]{2,0,1:T(4,128)(2,1)S(1)}, bf16[3,128,256]{2,0,1:T(4,128)(2,1)}, u32[]{:S(2)}, u32[]{:S(2)}) collective-permute-start(bf16[3,128,256]{2,0,1:T(4,128)(2,1)S(1)} %get-tuple-element.39), channel_id=1, source_target_pairs={{8,0},{16,8},{24,16},{32,24},{40,32},{48,40},{56,48},{64,56},{72,6... | collective-permute-start | bytes 589832 | tf_op jit(solution)/shard_map/ppermute | solution.py:22
  13.8 0.0 collective-permute-start
  13.8 0.8 fusion.22
  14.7 3.5 %collective-permute-start.3 = (bf16[3,256,128]{2,1,0:T(8,128)(2,1)}, bf16[3,256,128]{2,1,0:T(8,128)(2,1)}, u32[]{:S(2)}, u32[]{:S(2)}) collective-permute-start(bf16[3,256,128]{2,1,0:T(8,128)(2,1)} %get-tuple-element.41), channel_id=1, source_target_pairs={{1,0},{2,1},{3,2},{4,3},{5,4},{6,5},{7,6},{9,8},{10,9},{11,10},{12... | collective-permute-start | bytes 589832 | tf_op jit(solution)/shard_map/ppermute | solution.py:22
  18.2 1.3 collective-permute-start.2
  19.6 0.7 copy.17
  20.3 1.1 copy.16
  21.4 0.7 copy.11
  22.1 0.0 collective-permute-done.1
  22.1 2.1 %collective-permute-done = bf16[3,128,256]{2,0,1:T(4,128)(2,1)} collective-permute-done((bf16[3,128,256]{2,0,1:T(4,128)(2,1)S(1)}, bf16[3,128,256]{2,0,1:T(4,128)(2,1)}, u32[]{:S(2)}, u32[]{:S(2)}) %collective-permute-start) | collective-permute-done | bytes 196640 | tf_op jit(solution)/shard_map/ppermute | solution.py:21
  24.2 1.8 maximum_bitcast_fusion
  25.9 32.8 %gather_fusion = bf16[4096,3,256]{2,1,0:T(4,128)(2,1)} fusion(bf16[512,3,256]{2,1,0:T(4,128)(2,1)S(1)} %maximum_bitcast_fusion, s32[4096]{0:T(1024)S(1)} %broadcast_clamp_fusion), kind=kCustom, calls=%fused_computation | custom fusion | bytes 12599296 | tf_op jit(solution)/shard_map/jit(_take)/gather | solution.py:71
  58.7 9.2 %fusion.8 = bf16[3,3,256,256]{3,1,0,2:T(4,128)(2,1)S(1)} fusion(f32[3,3,16,256]{2,0,1,3:T(4,128)S(1)} %copy.17, f32[3,16,256]{1,0,2:T(4,128)S(1)} %copy-done.1, bf16[16,256,3,256]{3,2,1,0:T(4,128)(2,1)} %bitcast.42, pred[16,256]{0,1:T(8,128)(4,1)} %copy.11), kind=kOutput, calls=%fused_computation.11 | convolution fusion | flops 60579840 | bytes 7671808 | tf_op jit(solution)/shard_map/kcdna,nadi->kcai/dot_general | solution.py:75
  67.9 0.0 collective-permute-done.3
  67.9 0.0 collective-permute-done.2
  68.0 3.0 %convolution_bitcast_fusion = f32[3,512,256]{1,2,0:T(8,128)} fusion(bf16[3,3,256,256]{3,1,0,2:T(4,128)(2,1)S(1)} %fusion.8, bf16[3,256,128]{2,1,0:T(8,128)(2,1)} %collective-permute-done.3, bf16[3,256,256]{2,1,0:T(8,128)(2,1)S(1)} %copy-done, bf16[3,256,128]{2,1,0:T(8,128)(2,1)} %collective-permute-done.2), kind=kOutput, calls=%fused_computation.12 | convolution fusion | flops 606339072 | bytes 3538944 | tf_op jit(solution)/shard_map/caj,kcai->kji/dot_general | solution.py:79
  71.0 0.0 all-reduce.4.cloned.1.call-update
  71.0 0.6 copy-done.5
  71.6 8.7 %all-gather = f32[8,1,256]{2,1,0:T(1,128)S(1)} all-gather(f32[1,1,256]{2,1,0:T(1,128)S(1)} %bitcast.45), channel_id=1, replica_groups=mesh['atom'=16,'mode'=8] {'mode'}, dimensions={0}, use_global_device_ids=true | all-gather | bytes 9216 | tf_op jit(solution)/shard_map/all_gather | solution.py:64
  80.3 0.6 fusion.20
  82.3 0.6 dynamic-slice
  82.9 0.1 pad_dynamic-slice_fusion
  83.0 74.9 %all-reduce.4.cloned.1.call-done = f32[3,512,256]{1,2,0:T(8,128)} async-done(((f32[3,512,256]{1,2,0:T(8,128)}), f32[3,512,256]{1,2,0:T(8,128)}) %all-reduce.4.cloned.1.call-update) | async-done | bytes 1572880 | tf_op jit(solution)/shard_map/psum | solution.py:88
  157.8 1.6 multiply_reduce_fusion
  159.5 0.5 multiply_reduce_fusion.1
  160.0 0.6 multiply_bitcast_fusion
  160.6 0.3 reduce-window.9
  160.9 0.1 slice.34
  161.0 0.1 slice_reduce_fusion
  161.1 0.1 add_bitcast_fusion
  161.2 0.8 slice_dynamic-update-slice_fusion
  162.0 11.9 %all-reduce.1 = f32[8]{0:T(128)S(1)} all-reduce(f32[8]{0:T(128)S(1)} %slice_dynamic-update-slice_fusion), channel_id=1, replica_groups=mesh['atom'=16,'mode'=8] {'mode'}, use_global_device_ids=true, to_apply=%add.1 | all-reduce | flops 8 | bytes 64
  173.8 9.7 %while.10 = (s32[]{:T(128)}, f32[]{:T(128)}, s32[]{:T(128)}, f32[8]{0:T(128)S(1)}, s32[]{:T(128)}, /*index=5*/s32[]{:T(128)}, s32[]{:T(128)}) while((s32[]{:T(128)}, f32[]{:T(128)}, s32[]{:T(128)}, f32[8]{0:T(128)S(1)}, s32[]{:T(128)}, /*index=5*/s32[]{:T(128)}, s32[]{:T(128)}) %tuple.27), condition=%wide.region_8.9_spmd, body=%wide.region_7.8_spmd.sunk | while | flops 6 | bytes 143 | solution.py:35
  173.8 0.7 dynamic_slice.10
  175.2 0.7 dynamic_slice.10
  176.6 0.7 dynamic_slice.10
  178.0 0.7 dynamic_slice.10
  179.4 0.7 dynamic_slice.10
  180.8 0.7 dynamic_slice.10
  182.1 0.7 dynamic_slice.10
  183.5 0.6 add_multiply_fusion
  (21 shorter events, 0.1 us)
Async XLA Ops:
  7.2 6.7 %copy-start = (bf16[3,256,256]{2,1,0:T(8,128)(2,1)S(1)}, bf16[3,256,256]{2,1,0:T(8,128)(2,1)}, u32[]{:S(2)}) copy-start(bf16[3,256,256]{2,1,0:T(8,128)(2,1)} %param.8) | copy-start | bytes 1179652
  7.2 12.3 %copy-start.3 = (s32[16,256]{1,0:T(8,128)S(1)}, s32[16,256]{1,0:T(8,128)}, u32[]{:S(2)}) copy-start(s32[16,256]{1,0:T(8,128)} %param.11) | copy-start | bytes 49156
  7.2 12.4 %copy-start.2 = (f32[3,3,16,256]{3,2,1,0:T(8,128)S(1)}, f32[3,3,16,256]{3,2,1,0:T(8,128)}, u32[]{:S(2)}) copy-start(f32[3,3,16,256]{3,2,1,0:T(8,128)} %param.9) | copy-start | bytes 442372
  7.2 150.6 %all-reduce.4.cloned.1.call-start = ((), (), s32[]{:S(2)}) async-start(), calls=%async_computation | async-start | bytes 3145728 | tf_op jit(solution)/shard_map/psum | solution.py:88
  8.6 11.7 %copy-start.4 = (f32[3,16,256]{2,1,0:T(8,128)S(1)}, f32[3,16,256]{2,1,0:T(8,128)}, u32[]{:S(2)}) copy-start(f32[3,16,256]{2,1,0:T(8,128)} %param.10) | copy-start | bytes 147460
  8.8 13.3 %collective-permute-start.1 = (bf16[3,128,256]{2,0,1:T(4,128)(2,1)S(1)}, bf16[3,128,256]{2,0,1:T(4,128)(2,1)}, u32[]{:S(2)}, u32[]{:S(2)}) collective-permute-start(bf16[3,128,256]{2,0,1:T(4,128)(2,1)S(1)} %get-tuple-element.39), channel_id=1, source_target_pairs={{8,0},{16,8},{24,16},{32,24},{40,32},{48,40},{56,48},{64,56},{72,6... | collective-permute-start | bytes 589832 | tf_op jit(solution)/shard_map/ppermute | solution.py:22
  13.8 10.3 %collective-permute-start = (bf16[3,128,256]{2,0,1:T(4,128)(2,1)S(1)}, bf16[3,128,256]{2,0,1:T(4,128)(2,1)}, u32[]{:S(2)}, u32[]{:S(2)}) collective-permute-start(bf16[3,128,256]{2,0,1:T(4,128)(2,1)S(1)} %get-tuple-element.38), channel_id=1, source_target_pairs={{0,8},{8,16},{16,24},{24,32},{32,40},{40,48},{48,56},{56,64},{64,7... | collective-permute-start | bytes 589832 | tf_op jit(solution)/shard_map/ppermute | solution.py:21
  14.7 53.3 %collective-permute-start.3 = (bf16[3,256,128]{2,1,0:T(8,128)(2,1)}, bf16[3,256,128]{2,1,0:T(8,128)(2,1)}, u32[]{:S(2)}, u32[]{:S(2)}) collective-permute-start(bf16[3,256,128]{2,1,0:T(8,128)(2,1)} %get-tuple-element.41), channel_id=1, source_target_pairs={{1,0},{2,1},{3,2},{4,3},{5,4},{6,5},{7,6},{9,8},{10,9},{11,10},{12... | collective-permute-start | bytes 589832 | tf_op jit(solution)/shard_map/ppermute | solution.py:22
  18.2 49.7 %collective-permute-start.2 = (bf16[3,256,128]{2,1,0:T(8,128)(2,1)}, bf16[3,256,128]{2,1,0:T(8,128)(2,1)}, u32[]{:S(2)}, u32[]{:S(2)}) collective-permute-start(bf16[3,256,128]{2,1,0:T(8,128)(2,1)} %get-tuple-element.40), channel_id=1, source_target_pairs={{0,1},{1,2},{2,3},{3,4},{4,5},{5,6},{6,7},{8,9},{9,10},{10,11},{11... | collective-permute-start | bytes 589832 | tf_op jit(solution)/shard_map/ppermute | solution.py:21
  25.9 32.8 %copy-start.1 = (f32[3,16,256]{1,0,2:T(4,128)S(1)}, f32[3,16,256]{1,0,2:T(4,128)}, u32[]{:S(2)}) copy-start(f32[3,16,256]{1,0,2:T(4,128)} %copy.16) | copy-start | bytes 147460
  71.0 0.7 copy-start.5
  71.0 11.3 %copy-start.7 = (u32[128]{0:T(128)S(1)}, u32[128]{0:T(128)}, u32[]{:S(2)}) copy-start(u32[128]{0:T(128)} %constant.93) | copy-start | bytes 1540
  71.0 12.0 %copy-start.6 = (s32[2,256]{1,0:T(2,128)S(1)}, s32[2,256]{1,0:T(2,128)}, u32[]{:S(2)}) copy-start(s32[2,256]{1,0:T(2,128)} %param.12) | copy-start | bytes 6148
Sparse Core Ops, SparseCore 0:
  71.1 86.6 all-reduce.3
where the time goes:
time: 191 us
  waiting for transfers between devices  76.9 us (40%)
  local copies, waits for them, and re-layouts  44.7 us (23%)
  blocking collectives  20.6 us (11%)
  between operations  15.5 us (8%)
  matrix products  12.2 us (6%)
  starting transfers between devices  9.86 us (5%)
  other arithmetic  6.15 us (3%)
  loops' own time  5 us (3%)
    psum x1, waiting for transfers between devices, body(): summed_pair = lax.psum(pair_terms, 'atom')  74.9 us
    gather x1, local copies, waits for them, and re-layouts, body(): gathered = jnp.take(row_major, local_ids, axis=0)  32.8 us
    unnamed x1, blocking collectives  11.9 us
    dot_general x1, matrix products, body(): jnp.einsum('kcdna,nadi->kcai', coupling, gathered, preferred_element_type...  9.23 us
    all_gather x1, blocking collectives, body(): spectrum = lax.all_gather(freq, 'mode', axis=0, tiled=True)  8.7 us
    ppermute x2, starting transfers between devices, extended(): after = lax.ppermute(first, axis, down)  8.54 us
    unnamed x23, local copies, waits for them, and re-layouts  5.23 us
    another operation x1, loops' own time, prefix(): return lax.fori_loop(0, place, one, state)  5 us
  transfers between devices with their start and end apart: 5, of which 2 were waited for; matrix products, arithmetic and copies ran while one was open for 25% of the time, Pallas kernels for 0%

commit v1 on v0

--- a/solution.py
+++ b/solution.py
@@ -85,7 +85,11 @@
     partner_ids = mode_start - HALF + jnp.arange(partner_span, dtype=jnp.int32)
     own_ids = mode_start + jnp.arange(MODE_DEV, dtype=jnp.int32)
     weight = pair_weight(freq, partner_freq, own_ids, partner_ids, band[0], band[1], broaden)
-    summed_pair = lax.psum(pair_terms, "atom")
+    summed_pair = pair_terms
+    for hop in (1, 2, 4, 8):
+        summed_pair = summed_pair + lax.ppermute(
+            summed_pair, "atom", [(dev, dev ^ hop) for dev in range(16)]
+        )
     strength = jnp.sum(summed_pair * summed_pair, axis=0)
     row_sums = jnp.sum(weight * strength, axis=0)
     diffusivity = math.pi / (3.0 * freq * freq) * row_sums

time: 191 us -> 230 us (1.20)
  waiting for transfers between devices: 76.9 us -> 120 us
  between operations: 15.5 us -> 2.15 us
  blocking collectives: 20.6 us -> 29.4 us
  starting transfers between devices: 9.86 us -> 12.8 us
    ppermute x0 -> x4, waiting for transfers between devices: none -> 120 us  [body(): lax.ppermute(summed_pair, 'atom', [(dev, dev ^ hop) for dev in range(16)])]
    psum x1 -> x0, waiting for transfers between devices: 74.9 us -> none  [body(): summed_pair = lax.psum(pair_terms, 'atom')]
    unnamed x1, blocking collectives: 11.9 us -> 17 us
    all_gather x1, blocking collectives: 8.7 us -> 12.5 us  [body(): spectrum = lax.all_gather(freq, 'mode', axis=0, tiled=True)]
  transfers between devices with their start and end apart: 5 -> 8, of which waited for: 2 -> 4; matrix products, arithmetic and copies ran while one was open for 25% -> 21% of each run, Pallas kernels for 0% -> 0%
where the time goes in v1:
time: 230 us; the launch traced here: 229 us
  waiting for transfers between devices  120 us (52%)
  local copies, waits for them, and re-layouts  43.5 us (19%)
  blocking collectives  29.4 us (13%)
  starting transfers between devices  12.8 us (6%)
  matrix products  11.1 us (5%)
  other arithmetic  5.95 us (3%)
  loops' own time  4.12 us (2%)
    ppermute x4, waiting for transfers between devices, body(): lax.ppermute(summed_pair, 'atom', [(dev, dev ^ hop) for dev in range(16)])  120 us
    gather x1, local copies, waits for them, and re-layouts, body(): gathered = jnp.take(row_major, local_ids, axis=0)  32.8 us
    unnamed x1, blocking collectives  17 us
    all_gather x1, blocking collectives, body(): spectrum = lax.all_gather(freq, 'mode', axis=0, tiled=True)  12.5 us
    dot_general x1, matrix products, body(): jnp.einsum('kcdna,nadi->kcai', coupling, gathered, preferred_element_type...  9.23 us
    ppermute x2, starting transfers between devices, extended(): after = lax.ppermute(first, axis, down)  8.04 us
    unnamed x23, local copies, waits for them, and re-layouts  4.62 us
  transfers between devices with their start and end apart: 8, of which 4 were waited for; matrix products, arithmetic and copies ran while one was open for 21% of the time, Pallas kernels for 0%

profile of v1, /device:TPU:97, one launch (start us, length us, event | category | flops | bytes accessed | tf_op | source)
XLA Modules:
  0.0 229.4 jit_solution(5761367130808095341)
XLA Ops:
  0.7 1.4 copy.12
  2.1 0.2 fusion.21
  2.3 1.3 collective-permute-start
  3.5 3.8 %collective-permute-start.1 = (bf16[3,128,256]{2,0,1:T(4,128)(2,1)S(1)}, bf16[3,128,256]{2,0,1:T(4,128)(2,1)}, u32[]{:S(2)}, u32[]{:S(2)}) collective-permute-start(bf16[3,128,256]{2,0,1:T(4,128)(2,1)S(1)} %get-tuple-element.39), channel_id=1, source_target_pairs={{8,0},{16,8},{24,16},{32,24},{40,32},{48,40},{56,48},{64,56},{72,6... | collective-permute-start | bytes 589832 | tf_op jit(solution)/shard_map/ppermute | solution.py:22
  7.3 0.9 fusion.22
  8.2 1.3 collective-permute-start.2
  9.5 4.2 %collective-permute-start.3 = (bf16[3,256,128]{2,1,0:T(8,128)(2,1)}, bf16[3,256,128]{2,1,0:T(8,128)(2,1)}, u32[]{:S(2)}, u32[]{:S(2)}) collective-permute-start(bf16[3,256,128]{2,1,0:T(8,128)(2,1)} %get-tuple-element.41), channel_id=1, source_target_pairs={{1,0},{2,1},{3,2},{4,3},{5,4},{6,5},{7,6},{9,8},{10,9},{11,10},{12... | collective-permute-start | bytes 589832 | tf_op jit(solution)/shard_map/ppermute | solution.py:22
  13.8 0.7 copy.11
  14.5 0.7 copy.17
  15.3 1.1 copy.16
  16.3 1.8 maximum_bitcast_fusion
  18.1 32.8 %gather_fusion = bf16[4096,3,256]{2,1,0:T(4,128)(2,1)} fusion(bf16[512,3,256]{2,1,0:T(4,128)(2,1)S(1)} %maximum_bitcast_fusion, s32[4096]{0:T(1024)S(1)} %broadcast_clamp_fusion), kind=kCustom, calls=%fused_computation | custom fusion | bytes 12599296 | tf_op jit(solution)/shard_map/jit(_take)/gather | solution.py:71
  50.9 9.2 %fusion.8 = bf16[3,3,256,256]{3,1,0,2:T(4,128)(2,1)S(1)} fusion(f32[3,3,16,256]{2,0,1,3:T(4,128)S(1)} %copy.17, f32[3,16,256]{1,0,2:T(4,128)S(1)} %copy-done.1, bf16[16,256,3,256]{3,2,1,0:T(4,128)(2,1)} %bitcast.42, pred[16,256]{0,1:T(8,128)(4,1)} %copy.11), kind=kOutput, calls=%fused_computation.11 | convolution fusion | flops 60579840 | bytes 7671808 | tf_op jit(solution)/shard_map/kcdna,nadi->kcai/dot_general | solution.py:75
  60.1 1.8 convolution_bitcast_fusion
  62.0 0.1 collective-permute-start.4
  62.1 34.9 %collective-permute-done.4 = f32[3,512,256]{1,2,0:T(8,128)S(1)} collective-permute-done((f32[3,512,256]{1,2,0:T(8,128)S(1)}, f32[3,512,256]{1,2,0:T(8,128)S(1)}, u32[]{:S(2)}, u32[]{:S(2)}) %collective-permute-start.4) | collective-permute-done | bytes 1572896 | tf_op jit(solution)/shard_map/ppermute | solution.py:90
  96.9 0.3 add.106
  97.3 0.1 collective-permute-start.5
  97.4 35.5 %collective-permute-done.5 = f32[3,512,256]{1,2,0:T(8,128)S(1)} collective-permute-done((f32[3,512,256]{1,2,0:T(8,128)S(1)}, f32[3,512,256]{1,2,0:T(8,128)S(1)}, u32[]{:S(2)}, u32[]{:S(2)}) %collective-permute-start.5) | collective-permute-done | bytes 1572896 | tf_op jit(solution)/shard_map/ppermute | solution.py:90
  132.9 0.3 add.107
  133.2 0.0 copy-start.7
  133.3 0.2 collective-permute-start.6
  133.4 33.1 %collective-permute-done.6 = f32[3,512,256]{1,2,0:T(8,128)S(1)} collective-permute-done((f32[3,512,256]{1,2,0:T(8,128)S(1)}, f32[3,512,256]{1,2,0:T(8,128)S(1)}, u32[]{:S(2)}, u32[]{:S(2)}) %collective-permute-start.6) | collective-permute-done | bytes 1572896 | tf_op jit(solution)/shard_map/ppermute | solution.py:90
  166.5 0.3 add.108
  166.8 1.8 collective-permute-start.7
  168.7 12.5 %all-gather = f32[8,1,256]{2,1,0:T(1,128)S(1)} all-gather(f32[1,1,256]{2,1,0:T(1,128)S(1)} %bitcast.45), channel_id=1, replica_groups=mesh['atom'=16,'mode'=8] {'mode'}, dimensions={0}, use_global_device_ids=true | all-gather | bytes 9216 | tf_op jit(solution)/shard_map/all_gather | solution.py:64
  181.1 0.6 fusion.20
  183.0 0.6 dynamic-slice
  183.6 0.1 pad_dynamic-slice_fusion
  183.7 17.0 %collective-permute-done.7 = f32[3,512,256]{1,2,0:T(8,128)S(1)} collective-permute-done((f32[3,512,256]{1,2,0:T(8,128)S(1)}, f32[3,512,256]{1,2,0:T(8,128)S(1)}, u32[]{:S(2)}, u32[]{:S(2)}) %collective-permute-start.7) | collective-permute-done | bytes 1572896 | tf_op jit(solution)/shard_map/ppermute | solution.py:90
  200.7 0.4 multiply_reduce_fusion
  201.2 0.5 multiply_reduce_fusion.1
  201.7 0.6 multiply_bitcast_fusion
  202.3 0.3 reduce-window.9
  202.6 0.1 slice.34
  202.7 0.1 slice_reduce_fusion
  202.8 0.1 add_bitcast_fusion
  202.9 0.8 slice_dynamic-update-slice_fusion
  203.7 17.0 %all-reduce.1 = f32[8]{0:T(128)S(1)} all-reduce(f32[8]{0:T(128)S(1)} %slice_dynamic-update-slice_fusion), channel_id=1, replica_groups=mesh['atom'=16,'mode'=8] {'mode'}, use_global_device_ids=true, to_apply=%add.1 | all-reduce | flops 8 | bytes 64
  220.7 8.2 %while.10 = (s32[]{:T(128)}, f32[]{:T(128)}, s32[]{:T(128)}, f32[8]{0:T(128)S(1)}, s32[]{:T(128)}, /*index=5*/s32[]{:T(128)}, s32[]{:T(128)}) while((s32[]{:T(128)}, f32[]{:T(128)}, s32[]{:T(128)}, f32[8]{0:T(128)S(1)}, s32[]{:T(128)}, /*index=5*/s32[]{:T(128)}, s32[]{:T(128)}) %tuple.27), condition=%wide.region_7.8_spmd, body=%wide.region_6.7_spmd.sunk | while | flops 6 | bytes 135 | solution.py:35
  220.7 0.6 dynamic_slice.10
  221.8 0.6 dynamic_slice.10
  223.0 0.6 dynamic_slice.10
  224.2 0.6 dynamic_slice.10
  225.3 0.6 dynamic_slice.10
  226.5 0.6 dynamic_slice.10
  227.7 0.6 dynamic_slice.10
  228.8 0.6 add_multiply_fusion
  (29 shorter events, 0.2 us)
Async XLA Ops:
  0.6 6.7 %copy-start = (bf16[3,256,256]{2,1,0:T(8,128)(2,1)S(1)}, bf16[3,256,256]{2,1,0:T(8,128)(2,1)}, u32[]{:S(2)}) copy-start(bf16[3,256,256]{2,1,0:T(8,128)(2,1)} %param.8) | copy-start | bytes 1179652
  0.6 13.1 %copy-start.3 = (s32[16,256]{1,0:T(8,128)S(1)}, s32[16,256]{1,0:T(8,128)}, u32[]{:S(2)}) copy-start(s32[16,256]{1,0:T(8,128)} %param.11) | copy-start | bytes 49156
  0.6 13.9 %copy-start.2 = (f32[3,3,16,256]{3,2,1,0:T(8,128)S(1)}, f32[3,3,16,256]{3,2,1,0:T(8,128)}, u32[]{:S(2)}) copy-start(f32[3,3,16,256]{3,2,1,0:T(8,128)} %param.9) | copy-start | bytes 442372
  2.2 13.0 %copy-start.4 = (f32[3,16,256]{2,1,0:T(8,128)S(1)}, f32[3,16,256]{2,1,0:T(8,128)}, u32[]{:S(2)}) copy-start(f32[3,16,256]{2,1,0:T(8,128)} %param.10) | copy-start | bytes 147460
  2.3 14.1 %collective-permute-start = (bf16[3,128,256]{2,0,1:T(4,128)(2,1)S(1)}, bf16[3,128,256]{2,0,1:T(4,128)(2,1)}, u32[]{:S(2)}, u32[]{:S(2)}) collective-permute-start(bf16[3,128,256]{2,0,1:T(4,128)(2,1)S(1)} %get-tuple-element.38), channel_id=1, source_target_pairs={{0,8},{8,16},{16,24},{24,32},{32,40},{40,48},{48,56},{56,64},{64,7... | collective-permute-start | bytes 589832 | tf_op jit(solution)/shard_map/ppermute | solution.py:21
  3.5 12.8 %collective-permute-start.1 = (bf16[3,128,256]{2,0,1:T(4,128)(2,1)S(1)}, bf16[3,128,256]{2,0,1:T(4,128)(2,1)}, u32[]{:S(2)}, u32[]{:S(2)}) collective-permute-start(bf16[3,128,256]{2,0,1:T(4,128)(2,1)S(1)} %get-tuple-element.39), channel_id=1, source_target_pairs={{8,0},{16,8},{24,16},{32,24},{40,32},{48,40},{56,48},{64,56},{72,6... | collective-permute-start | bytes 589832 | tf_op jit(solution)/shard_map/ppermute | solution.py:22
  8.2 51.9 %collective-permute-start.2 = (bf16[3,256,128]{2,1,0:T(8,128)(2,1)}, bf16[3,256,128]{2,1,0:T(8,128)(2,1)}, u32[]{:S(2)}, u32[]{:S(2)}) collective-permute-start(bf16[3,256,128]{2,1,0:T(8,128)(2,1)} %get-tuple-element.40), channel_id=1, source_target_pairs={{0,1},{1,2},{2,3},{3,4},{4,5},{5,6},{6,7},{8,9},{9,10},{10,11},{11... | collective-permute-start | bytes 589832 | tf_op jit(solution)/shard_map/ppermute | solution.py:21
  9.5 50.6 %collective-permute-start.3 = (bf16[3,256,128]{2,1,0:T(8,128)(2,1)}, bf16[3,256,128]{2,1,0:T(8,128)(2,1)}, u32[]{:S(2)}, u32[]{:S(2)}) collective-permute-start(bf16[3,256,128]{2,1,0:T(8,128)(2,1)} %get-tuple-element.41), channel_id=1, source_target_pairs={{1,0},{2,1},{3,2},{4,3},{5,4},{6,5},{7,6},{9,8},{10,9},{11,10},{12... | collective-permute-start | bytes 589832 | tf_op jit(solution)/shard_map/ppermute | solution.py:22
  18.1 32.8 %copy-start.1 = (f32[3,16,256]{1,0,2:T(4,128)S(1)}, f32[3,16,256]{1,0,2:T(4,128)}, u32[]{:S(2)}) copy-start(f32[3,16,256]{1,0,2:T(4,128)} %copy.16) | copy-start | bytes 147460
  62.0 35.0 %collective-permute-start.4 = (f32[3,512,256]{1,2,0:T(8,128)S(1)}, f32[3,512,256]{1,2,0:T(8,128)S(1)}, u32[]{:S(2)}, u32[]{:S(2)}) collective-permute-start(f32[3,512,256]{1,2,0:T(8,128)S(1)} %convolution_bitcast_fusion), channel_id=1, source_target_pairs={{0,8},{8,0},{16,24},{24,16},{32,40},{40,32},{48,56},{56,48},{64,72... | collective-permute-start | bytes 4718600 | tf_op jit(solution)/shard_map/ppermute | solution.py:90
  97.3 35.6 %collective-permute-start.5 = (f32[3,512,256]{1,2,0:T(8,128)S(1)}, f32[3,512,256]{1,2,0:T(8,128)S(1)}, u32[]{:S(2)}, u32[]{:S(2)}) collective-permute-start(f32[3,512,256]{1,2,0:T(8,128)S(1)} %add.106), channel_id=1, source_target_pairs={{0,16},{8,24},{16,0},{24,8},{32,48},{40,56},{48,32},{56,40},{64,80... | collective-permute-start | bytes 4718600 | tf_op jit(solution)/shard_map/ppermute | solution.py:90
  133.2 35.4 %copy-start.5 = (f32[256]{0:T(256)S(1)}, f32[256]{0:T(256)}, u32[]{:S(2)}) copy-start(f32[256]{0:T(256)} %param.13) | copy-start | bytes 3076
  133.2 49.8 %copy-start.7 = (u32[128]{0:T(128)S(1)}, u32[128]{0:T(128)}, u32[]{:S(2)}) copy-start(u32[128]{0:T(128)} %constant.93) | copy-start | bytes 1540
  133.2 50.5 %copy-start.6 = (s32[2,256]{1,0:T(2,128)S(1)}, s32[2,256]{1,0:T(2,128)}, u32[]{:S(2)}) copy-start(s32[2,256]{1,0:T(2,128)} %param.12) | copy-start | bytes 6148
  133.3 33.2 %collective-permute-start.6 = (f32[3,512,256]{1,2,0:T(8,128)S(1)}, f32[3,512,256]{1,2,0:T(8,128)S(1)}, u32[]{:S(2)}, u32[]{:S(2)}) collective-permute-start(f32[3,512,256]{1,2,0:T(8,128)S(1)} %add.107), channel_id=1, source_target_pairs={{0,32},{8,40},{16,48},{24,56},{32,0},{40,8},{48,16},{56,24},{64,96... | collective-permute-start | bytes 4718600 | tf_op jit(solution)/shard_map/ppermute | solution.py:90
  166.8 33.9 %collective-permute-start.7 = (f32[3,512,256]{1,2,0:T(8,128)S(1)}, f32[3,512,256]{1,2,0:T(8,128)S(1)}, u32[]{:S(2)}, u32[]{:S(2)}) collective-permute-start(f32[3,512,256]{1,2,0:T(8,128)S(1)} %add.108), channel_id=1, source_target_pairs={{0,64},{8,72},{16,80},{24,88},{32,96},{40,104},{48,112},{56,120},{... | collective-permute-start | bytes 4718600 | tf_op jit(solution)/shard_map/ppermute | solution.py:90
